TPU v7x, 32 devices: a whole 2x2x4 slice. The times are simulated.
32 devices in a mesh: grp: 2 (over x), tm: 16 (over z, y, core).
Axes of the slice: x: 2, y: 2, z: 4, core: 2. Of those that a mesh axis runs over, the one named last changes fastest.
Arguments:
- frames_in: bfloat16 [16384, 1536], P(('grp', 'tm')), parts along dimension 0, may hold values from -6 to 6
- frame_time: int32 [64], P('grp'), parts along dimension 0, may hold values from 0 to 31, each once
- norm_gain: float32 [1536], replicated, may hold values from 0.25 to 1.75
- w_query: bfloat16 [1536, 768], replicated, may hold values from -2 to 2
- w_key: bfloat16 [1536, 768], replicated, may hold values from -2 to 2
- w_value: bfloat16 [1536, 768], replicated, may hold values from -0.15625 to 0.15625
- w_output: bfloat16 [768, 1536], replicated, may hold values from -0.21875 to 0.21875
Outputs:
- attended: bfloat16 [16384, 1536], P(('grp', 'tm')), parts along dimension 0
There are 2 independent parts, one for each index of `grp`. A program takes and returns all parts, laid end to end along the dimension named above; an argument that names none is the same for every part. Nothing has to cross between parts.
Inputs may be any that keep to these rules, and one draw needn't show every extreme that they name: `frame_time`: each of 0 to 31 stands once.
All inputs are finite; a program needn't handle non-finite values.
Results may differ from a plain program's by a relative error of at most 0.004.
The roundings to bfloat16 on the way count: a program that leaves them out, or rounds other values in their place, can miss the bound.
Values may be sent and summed in bfloat16 or wider, within the bound.
A program may use at most 128 MiB of HBM per device.

v0:
```python
import functools

import jax
import jax.numpy as jnp
from jax import lax
from jax.experimental import pallas as pl
from jax.experimental.pallas import tpu as pltpu
from jax.sharding import PartitionSpec as P

HEADS = 6
HD = 128
HH = 16
WW = 16
WIN = 8
POOL = 4
TOKENS = HH * WW
PK = (HH // POOL) * (WW // POOL)
HALF = WIN * WW
NEG = -1e30
LOG2E = 1.4426950408889634
MESH = pl.DeviceIdType.MESH
NT = (((1,), (1,)), ((), ()))


def kernel(n, snake, near_reach, ft, gain, x_hbm, wq_hbm, wk_hbm, wv_hbm, mixed,
           x_v, wq, wk, wv, normed, q_s, k_s, v_s, far, bias, top_s, acc_s, s_s, p_s,
           x_sem, w_sem, ring_send, ring_recv, sib_send, sib_recv):
    rows = x_v.shape[0]
    count = rows // TOKENS
    own = count * PK
    pieces, keys, tile = far.shape
    parts = pieces // 2
    chips = n // 2
    me = lax.axis_index("tm")
    core = me % 2
    chip = me // 2
    half = chips // 2
    reach = (chips // 2, (chips - 1) // 2)

    def chip_at(pos):
        pos = (pos + chips) % chips
        if not snake:
            return pos
        side = pos // half
        return (1 - side) * (2 * pos) + side * (2 * (chips - 1 - pos) + 1)

    if snake:
        place = (1 - chip % 2) * (chip // 2) + (chip % 2) * (chips - 1 - chip // 2)
    else:
        place = chip
    sibling = chip * 2 + (1 - core)
    step_of = (1, -1)
    neighbour = [[chip_at(place + s * jump) * 2 + core for jump in (1, 2)] for s in step_of]

    def limit(way, piece):
        return reach[way] if piece < parts else reach[1 - way]

    def place_of(way, dist, cross):
        if dist == 0:
            return cross * own
        first = (4 * dist - 2) * own
        if 2 * dist == chips:
            return first + cross * own
        return first + (2 * way + cross) * own

    blocks = x_sem.shape[0]
    size = rows // blocks
    loads = []
    for b in range(blocks):
        part = pl.ds(b * size, size)
        loads.append(pltpu.make_async_copy(x_hbm.at[part], x_v.at[part], x_sem.at[b]))
        loads[-1].start()
    weights = []
    for i, (src, dst) in enumerate(((wk_hbm, wk), (wv_hbm, wv), (wq_hbm, wq))):
        weights.append(pltpu.make_async_copy(src, dst, w_sem.at[i]))
        weights[-1].start()

    barrier = pltpu.get_barrier_semaphore()
    for other in (*neighbour[0], *neighbour[1], sibling):
        pl.semaphore_signal(barrier, inc=1, device_id={"tm": other}, device_id_type=MESH)

    sub = 32
    for b in range(blocks):
        loads[b].wait()

        def norm(i, carry, b=b):
            part = pl.ds(pl.multiple_of(b * size + i * sub, sub), sub)
            xf = x_v[part, :].astype(jnp.float32)
            scale = lax.rsqrt(jnp.mean(xf * xf, axis=-1, keepdims=True) + 1e-06)
            normed[part, :] = (xf * scale * gain[...]).astype(jnp.bfloat16)
            return carry

        lax.fori_loop(0, size // sub, norm, 0)

    pr = lax.broadcasted_iota(jnp.int32, (own, rows), 0)
    pc = lax.broadcasted_iota(jnp.int32, (own, rows), 1)
    block_of = (pc // TOKENS) * PK + (pc % TOKENS) // (POOL * WW) * (WW // POOL) + (pc % WW) // POOL
    pool = jnp.where(pr == block_of, 1.0 / (POOL * POOL), 0.0).astype(jnp.bfloat16)

    def ring(way, dist, to, piece):
        return pltpu.make_async_remote_copy(
            src_ref=far.at[piece, pl.ds(place_of(way, dist, 0), own)],
            dst_ref=far.at[piece, pl.ds(place_of(way, to, 0), own)],
            send_sem=ring_send.at[way, to - 1, piece], recv_sem=ring_recv.at[way, to - 1, piece],
            device_id={"tm": neighbour[way][to - dist - 1]}, device_id_type=MESH)

    def across(way, dist, piece):
        return pltpu.make_async_remote_copy(
            src_ref=far.at[piece, pl.ds(place_of(way, dist, 0), own)],
            dst_ref=far.at[piece, pl.ds(place_of(way, dist, 1), own)],
            send_sem=sib_send.at[way, dist, piece], recv_sem=sib_recv.at[way, dist, piece],
            device_id={"tm": sibling}, device_id_type=MESH)

    sends = []
    incoming = {}

    def send(way, dist, piece):
        for to in (dist + 2, dist + 1):
            if dist % 2 == 0 and to <= limit(way, piece):
                copy = ring(way, dist, to, piece)
                copy.start()
                sends.append(copy)

    def share(way, dist, piece):
        copy = across(way, dist, piece)
        copy.start()
        sends.append(copy)
        incoming.setdefault(dist, []).append(copy)

    def relay(dist):
        for piece in range(pieces):
            for way in (0, 1):
                if dist <= limit(way, piece):
                    ring(way, (dist - 1) // 2 * 2, dist, piece).wait_recv()
                    send(way, dist, piece)
                    share(way, dist, piece)

    def settle(dists):
        for dist in dists:
            for copy in incoming.get(dist, ()):
                copy.wait_recv()

    def project(w, out, j):
        cols = pl.ds(j * tile, tile)
        out[:, cols] = jnp.dot(
            normed[...], w[:, cols], preferred_element_type=jnp.float32
        ).astype(jnp.bfloat16)

    for base, weight, w, out in ((0, weights[0], wk, k_s), (parts, weights[1], wv, v_s)):
        weight.wait()
        for j in range(parts):
            project(w, out, j)
            far[base + j, pl.ds(0, own), :] = jnp.dot(
                pool, out[:, pl.ds(j * tile, tile)], preferred_element_type=jnp.float32
            ).astype(jnp.bfloat16)
            if base + j == 0:
                pl.semaphore_wait(barrier, 5)
            for way in (0, 1):
                send(way, 0, base + j)
            share(0, 0, base + j)

    slot = lax.broadcasted_iota(jnp.int32, (1, keys), 1) // PK
    key_time = jnp.zeros((1, keys), jnp.int32)
    for dist in range(reach[0] + 1):
        for way in (0, 1):
            if (dist == 0 or 2 * dist == chips) and way == 1:
                continue
            for cross in (0, 1):
                plane = core * (1 - cross) + (1 - core) * cross
                dev = chip_at(place - step_of[way] * dist) * 2 + plane
                first = place_of(way, dist, cross) // PK
                for f in range(count):
                    key_time = jnp.where(slot == first + f, ft[dev * count + f], key_time)
    for f in range(count):
        bias[f] = jnp.where(key_time < ft[me * count + f], 0.0, NEG)

    weights[2].wait()
    for j in range(parts):
        project(wq, q_s, j)

    ir = lax.broadcasted_iota(jnp.int32, (HALF, HALF), 0)
    ic = lax.broadcasted_iota(jnp.int32, (HALF, HALF), 1)
    near_bias = jnp.where((ir // WIN) % 2 == (ic // WIN) % 2, 0.0, NEG)
    rate = LOG2E / HD**0.5
    cut = min(keys, (4 * near_reach + 2) * own)
    groups = tile // HD

    ones = jnp.ones((1, HD), jnp.bfloat16)

    def with_ones(v):
        return jnp.concatenate([v, jnp.broadcast_to(ones, v.shape)], axis=1)

    def attend(h, lo, size, first, last):
        cols = pl.ds(pl.multiple_of(h * HD, HD), HD)
        inner = pl.ds(pl.multiple_of(h % groups * HD, HD), HD)
        span = pl.ds(0, size)
        k_far = far[h // groups, pl.ds(lo, size), inner]
        v_far = far[parts + h // groups, pl.ds(lo, size), inner]
        s_s[:, span] = lax.dot_general(q_s[:, cols], k_far, NT, preferred_element_type=jnp.float32)
        near = []
        keeps = []
        for block in range(rows // HALF):
            here = pl.ds(block * HALF, HALF)
            s = s_s[here, span] + bias[block * HALF // TOKENS, :, pl.ds(lo, size)]
            if first:
                s0 = lax.dot_general(q_s[here, cols], k_s[here, cols], NT, preferred_element_type=jnp.float32)
                s = jnp.concatenate([s0 + near_bias, s], axis=1)
            top = jnp.broadcast_to(jnp.max(s, -1, keepdims=True), (HALF, HD))
            if not first:
                old = top_s[h, here, :]
                top = jnp.maximum(old, top)
                keeps.append(jnp.exp2((old - top) * rate))
            if not last:
                top_s[h, here, :] = top
            w = jnp.exp2((s - jnp.tile(top, (1, -(-s.shape[1] // HD)))[:, :s.shape[1]]) * rate).astype(jnp.bfloat16)
            if first:
                near.append(jnp.dot(w[:, :HD], with_ones(v_s[here, cols]), preferred_element_type=jnp.float32))
                w = w[:, HD:]
            p_s[here, span] = w
        acc = jnp.dot(p_s[:, span], with_ones(v_far), preferred_element_type=jnp.float32)
        for block in range(rows // HALF):
            here = pl.ds(block * HALF, HALF)
            mine = acc[block * HALF:(block + 1) * HALF]
            if first:
                mine = mine + near[block]
            else:
                mine = mine + acc_s[h, here, :] * jnp.tile(keeps[block], (1, 2))
            if last:
                mixed[here, cols] = (mine[:, :HD] / mine[:, HD:]).astype(jnp.bfloat16)
            else:
                acc_s[h, here, :] = mine

    def first_pass(h, carry):
        attend(h, 0, cut, True, cut == keys)
        return carry

    def second_pass(h, carry):
        attend(h, cut, keys - cut, False, True)
        return carry

    for dist in range(1, near_reach + 1):
        relay(dist)
    settle(range(near_reach + 1))
    later = list(range(near_reach + 1, reach[0] + 1))
    spread = HEADS // 2
    lax.fori_loop(0, spread, first_pass, 0)
    for dist in later[:1]:
        relay(dist)
    lax.fori_loop(spread, HEADS, first_pass, 0)
    for dist in later[1:]:
        relay(dist)
    settle(later)
    if cut < keys:
        lax.fori_loop(0, HEADS, second_pass, 0)
    for copy in sends:
        copy.wait_send()


def on_device(n, snake, frames_in, frame_time, norm_gain, w_query, w_key, w_value, w_output):
    rows, width = frames_in.shape
    inner = w_query.shape[1]
    count = rows // TOKENS
    keys = n * count * PK
    hops = n // 4 + 1
    tile = 2 * HD
    pieces = 2 * (inner // tile)
    near_reach = n // 8
    bf = jnp.bfloat16
    f32 = jnp.float32
    dma = pltpu.SemaphoreType.DMA
    hbm = pl.BlockSpec(memory_space=pl.ANY)
    vmem = pl.BlockSpec(memory_space=pltpu.VMEM)
    mixed = pl.pallas_call(
        functools.partial(kernel, n, snake, near_reach),
        out_shape=jax.ShapeDtypeStruct((rows, inner), bf),
        in_specs=[pl.BlockSpec(memory_space=pltpu.SMEM), vmem, hbm, hbm, hbm, hbm],
        out_specs=vmem,
        scratch_shapes=[
            pltpu.VMEM((rows, width), bf),
            pltpu.VMEM((width, inner), bf),
            pltpu.VMEM((width, inner), bf),
            pltpu.VMEM((width, inner), bf),
            pltpu.VMEM((rows, width), bf),
            pltpu.VMEM((rows, inner), bf),
            pltpu.VMEM((rows, inner), bf),
            pltpu.VMEM((rows, inner), bf),
            pltpu.VMEM((pieces, keys, tile), bf),
            pltpu.VMEM((count, 1, keys), f32),
            pltpu.VMEM((HEADS, rows, HD), f32),
            pltpu.VMEM((HEADS, rows, 2 * HD), f32),
            pltpu.VMEM((rows, keys), f32),
            pltpu.VMEM((rows, keys), bf),
            dma((4,)),
            dma((3,)),
            dma((2, hops, pieces)),
            dma((2, hops, pieces)),
            dma((2, hops, pieces)),
            dma((2, hops, pieces)),
        ],
        compiler_params=pltpu.CompilerParams(
            collective_id=0, has_side_effects=True, vmem_limit_bytes=56 << 20
        ),
    )(frame_time, norm_gain, frames_in, w_query, w_key, w_value)
    return jnp.dot(mixed, w_output, preferred_element_type=f32).astype(bf)


def is_snake(mesh):
    names = list(mesh.axis_names)
    line = mesh.devices.transpose(names.index("grp"), names.index("tm"))[0]
    try:
        second = {d.coords[1] for d in line}
        third = {d.coords[2] for d in line}
    except (AttributeError, TypeError):
        return False
    return len(second) == 2 and len(third) * 4 == len(line)


def solution(mesh):
    placed = (P(("grp", "tm"), None), P("grp"), P(), P(), P(), P(), P())
    n = mesh.shape["tm"]
    return jax.shard_map(
        functools.partial(on_device, n, is_snake(mesh)),
        mesh=mesh, in_specs=placed, out_specs=P(("grp", "tm"), None), check_vma=False,
    )
```

profile of v0, /device:TPU:1, one launch (start us, length us, event | category | flops | bytes accessed | tf_op | source)
XLA Modules:
  0.0 36.1 jit_solution(7573024549136993860)
XLA Ops:
  0.0 0.0 copy-start
  0.0 32.4 %shard_map.73 = bf16[512,768]{1,0:T(8,128)(2,1)} custom-call(s32[32]{0:T(128)} %ft.1, f32[1536]{0:T(1024)} %gain.1, bf16[512,1536]{1,0:T(8,128)(2,1)} %x_hbm.1, bf16[1536,768]{1,0:T(8,128)(2,1)} %wq_hbm.1, bf16[1536,768]{1,0:T(8,128)(2,1)} %wk_hbm.1, bf16[1536,768]{1,0:T(8,128)(2,1)} %wv_hbm.1), custom_call_target="tpu_custom_call" | custom-call | tf_op jit(solution)/shard_map/pallas_call | solution.py:273
  32.4 0.0 copy-done
  32.4 3.7 %convolution_convert_fusion = bf16[512,1536]{1,0:T(8,128)(2,1)} fusion(bf16[512,768]{1,0:T(8,128)(2,1)} %shard_map.73, bf16[768,1536]{1,0:T(8,128)(2,1)S(1)} %copy-done), kind=kOutput, calls=%fused_computation | convolution fusion | flops 1208745984 | bytes 4718592 | tf_op jit(solution)/shard_map/dot_general | solution.py:304
Async XLA Ops:
  0.0 32.4 %copy-start = (bf16[768,1536]{1,0:T(8,128)(2,1)S(1)}, bf16[768,1536]{1,0:T(8,128)(2,1)}, u32[]{:S(2)}) copy-start(bf16[768,1536]{1,0:T(8,128)(2,1)} %param.13) | copy-start | bytes 7077892
where the time goes:
time: 36.3 us; the launch traced here: 36.1 us
  Pallas kernels  32.4 us (89%)
  matrix products  3.67 us (10%)
    pallas_call x1, Pallas kernels, on_device(): pl.pallas_call(functools.partial(kernel, n, snake, near_reach), out_shape...  32.4 us
    dot_general x1, matrix products, on_device(): return jnp.dot(mixed, w_output, preferred_element_type=f32).astype(bf)  3.67 us

commit v1 on v0

--- a/solution.py
+++ b/solution.py
@@ -22,7 +22,7 @@
 NT = (((1,), (1,)), ((), ()))
 
 
-def kernel(n, snake, near_reach, ft, gain, x_hbm, wq_hbm, wk_hbm, wv_hbm, mixed,
+def kernel(n, snake, near_reach, ft, gain, x_hbm, wq_hbm, wk_hbm, wv_hbm, wo_hbm, mixed, wo,
            x_v, wq, wk, wv, normed, q_s, k_s, v_s, far, bias, top_s, acc_s, s_s, p_s,
            x_sem, w_sem, ring_send, ring_recv, sib_send, sib_recv):
     rows = x_v.shape[0]
@@ -71,7 +71,7 @@
         loads.append(pltpu.make_async_copy(x_hbm.at[part], x_v.at[part], x_sem.at[b]))
         loads[-1].start()
     weights = []
-    for i, (src, dst) in enumerate(((wk_hbm, wk), (wv_hbm, wv), (wq_hbm, wq))):
+    for i, (src, dst) in enumerate(((wk_hbm, wk), (wv_hbm, wv), (wq_hbm, wq), (wo_hbm, wo))):
         weights.append(pltpu.make_async_copy(src, dst, w_sem.at[i]))
         weights[-1].start()
 
@@ -140,24 +140,24 @@
             for copy in incoming.get(dist, ()):
                 copy.wait_recv()
 
-    def project(w, out, j):
-        cols = pl.ds(j * tile, tile)
-        out[:, cols] = jnp.dot(
-            normed[...], w[:, cols], preferred_element_type=jnp.float32
-        ).astype(jnp.bfloat16)
-
-    for base, weight, w, out in ((0, weights[0], wk, k_s), (parts, weights[1], wv, v_s)):
+    means = jnp.dot(pool, normed[...], preferred_element_type=jnp.float32).astype(jnp.bfloat16)
+    for base, weight, w in ((0, weights[0], wk), (parts, weights[1], wv)):
         weight.wait()
         for j in range(parts):
-            project(w, out, j)
             far[base + j, pl.ds(0, own), :] = jnp.dot(
-                pool, out[:, pl.ds(j * tile, tile)], preferred_element_type=jnp.float32
+                means, w[:, pl.ds(j * tile, tile)], preferred_element_type=jnp.float32
             ).astype(jnp.bfloat16)
             if base + j == 0:
                 pl.semaphore_wait(barrier, 5)
             for way in (0, 1):
                 send(way, 0, base + j)
             share(0, 0, base + j)
+
+    def project(w, out):
+        out[...] = jnp.dot(normed[...], w[...], preferred_element_type=jnp.float32).astype(jnp.bfloat16)
+
+    project(wk, k_s)
+    project(wv, v_s)
 
     slot = lax.broadcasted_iota(jnp.int32, (1, keys), 1) // PK
     key_time = jnp.zeros((1, keys), jnp.int32)
@@ -175,8 +175,7 @@
         bias[f] = jnp.where(key_time < ft[me * count + f], 0.0, NEG)
 
     weights[2].wait()
-    for j in range(parts):
-        project(wq, q_s, j)
+    project(wq, q_s)
 
     ir = lax.broadcasted_iota(jnp.int32, (HALF, HALF), 0)
     ic = lax.broadcasted_iota(jnp.int32, (HALF, HALF), 1)
@@ -254,6 +253,19 @@
         lax.fori_loop(0, HEADS, second_pass, 0)
     for copy in sends:
         copy.wait_send()
+    weights[3].wait()
+
+
+def finish(mixed, wo, out_hbm, out_v, sem):
+    chunks, rows, width = out_v.shape
+    copies = []
+    for c in range(chunks):
+        cols = pl.ds(c * width, width)
+        out_v[c] = jnp.dot(mixed[...], wo[:, cols], preferred_element_type=jnp.float32).astype(jnp.bfloat16)
+        copies.append(pltpu.make_async_copy(out_v.at[c], out_hbm.at[:, cols], sem.at[c]))
+        copies[-1].start()
+    for copy in copies:
+        copy.wait()
 
 
 def on_device(n, snake, frames_in, frame_time, norm_gain, w_query, w_key, w_value, w_output):
@@ -270,11 +282,11 @@
     dma = pltpu.SemaphoreType.DMA
     hbm = pl.BlockSpec(memory_space=pl.ANY)
     vmem = pl.BlockSpec(memory_space=pltpu.VMEM)
-    mixed = pl.pallas_call(
+    mixed, wo = pl.pallas_call(
         functools.partial(kernel, n, snake, near_reach),
-        out_shape=jax.ShapeDtypeStruct((rows, inner), bf),
-        in_specs=[pl.BlockSpec(memory_space=pltpu.SMEM), vmem, hbm, hbm, hbm, hbm],
-        out_specs=vmem,
+        out_shape=(pltpu.VMEM((rows, inner), bf), pltpu.VMEM((inner, width), bf)),
+        in_specs=[pl.BlockSpec(memory_space=pltpu.SMEM), vmem, hbm, hbm, hbm, hbm, hbm],
+        out_specs=(vmem, vmem),
         scratch_shapes=[
             pltpu.VMEM((rows, width), bf),
             pltpu.VMEM((width, inner), bf),
@@ -291,17 +303,25 @@
             pltpu.VMEM((rows, keys), f32),
             pltpu.VMEM((rows, keys), bf),
             dma((4,)),
-            dma((3,)),
+            dma((4,)),
             dma((2, hops, pieces)),
             dma((2, hops, pieces)),
             dma((2, hops, pieces)),
             dma((2, hops, pieces)),
         ],
         compiler_params=pltpu.CompilerParams(
-            collective_id=0, has_side_effects=True, vmem_limit_bytes=56 << 20
+            collective_id=0, has_side_effects=True, vmem_limit_bytes=60 << 20
         ),
-    )(frame_time, norm_gain, frames_in, w_query, w_key, w_value)
-    return jnp.dot(mixed, w_output, preferred_element_type=f32).astype(bf)
+    )(frame_time, norm_gain, frames_in, w_query, w_key, w_value, w_output)
+    chunks = width // (4 * HD)
+    return pl.pallas_call(
+        finish,
+        out_shape=jax.ShapeDtypeStruct((rows, width), bf),
+        in_specs=[vmem, vmem],
+        out_specs=hbm,
+        scratch_shapes=[pltpu.VMEM((chunks, rows, width // chunks), bf), dma((chunks,))],
+        compiler_params=pltpu.CompilerParams(vmem_limit_bytes=8 << 20),
+    )(mixed, wo)
 
 
 def is_snake(mesh):

time: 36.3 us -> 33 us (0.909)
  matrix products: 3.67 us -> 0 us
    dot_general x1 -> x0, matrix products: 3.67 us -> none  [on_device(): return jnp.dot(mixed, w_output, preferred_element_type=f32).astype(bf)]
    pallas_call x0 -> x1, Pallas kernels: none -> 2.21 us  [on_device(): pl.pallas_call(finish, out_shape=jax.ShapeDtypeStruct((rows, width), bf),...]
    pallas_call x1, Pallas kernels: 32.4 us -> 30.2 us  [on_device(): pl.pallas_call(functools.partial(kernel, n, snake, near_reach), out_shape...]
where the time goes in v1:
time: 33 us; the launch traced here: 32.4 us
  Pallas kernels  32.4 us (98%)
    pallas_call x1, Pallas kernels, on_device(): pl.pallas_call(functools.partial(kernel, n, snake, near_reach), out_shape...  30.2 us
    pallas_call x1, Pallas kernels, on_device(): pl.pallas_call(finish, out_shape=jax.ShapeDtypeStruct((rows, width), bf),...  2.21 us

profile of v1, /device:TPU:1, one launch (start us, length us, event | category | flops | bytes accessed | tf_op | source)
XLA Modules:
  0.0 32.4 jit_solution(1489751094888648693)
XLA Ops:
  0.0 30.2 %shard_map.73 = (bf16[512,768]{1,0:T(8,128)(2,1)S(1)}, bf16[768,1536]{1,0:T(8,128)(2,1)S(1)}) custom-call(s32[32]{0:T(128)} %ft.1, f32[1536]{0:T(1024)} %gain.1, bf16[512,1536]{1,0:T(8,128)(2,1)} %x_hbm.1, bf16[1536,768]{1,0:T(8,128)(2,1)} %wq_hbm.1, bf16[1536,768]{1,0:T(8,128)(2,1)} %wk_hbm.1, bf16[1536,768]{1,0:T(8,128)(2,1)} %wv_hbm.1, ...), custom_call_target="tpu_custom_call" | custom-call | tf_op jit(solution)/shard_map/pallas_call | solution.py:285
  30.2 2.2 %shard_map.74 = bf16[512,1536]{1,0:T(8,128)(2,1)} custom-call(bf16[512,768]{1,0:T(8,128)(2,1)S(1)} %get-tuple-element.7.mixed, bf16[768,1536]{1,0:T(8,128)(2,1)S(1)} %get-tuple-element.8.wo), custom_call_target="tpu_custom_call" | custom-call | tf_op jit(solution)/shard_map/pallas_call | solution.py:317

commit v2 on v1

v2 whole, which is shorter than its diff:
```python
import functools

import jax
import jax.numpy as jnp
from jax import lax
from jax.experimental import pallas as pl
from jax.experimental.pallas import tpu as pltpu
from jax.sharding import PartitionSpec as P

HEADS = 6
HD = 128
HH = 16
WW = 16
WIN = 8
POOL = 4
TOKENS = HH * WW
PK = (HH // POOL) * (WW // POOL)
HALF = WIN * WW
NEG = -1e30
LOG2E = 1.4426950408889634
MESH = pl.DeviceIdType.MESH
NT = (((1,), (1,)), ((), ()))


def kernel(n, snake, cut, ft_hbm, gain_hbm, x_hbm, wq_hbm, wk_hbm, wv_hbm, wo_hbm, mixed, wo,
           ft, gain, x_v, wq, wk, wv, normed, q_s, k_s, v_s, far, bias, top_s, acc_s, s_s, p_all,
           x_sem, w_sem, small_sem, send_sem, recv_sem, sib_send, sib_recv):
    rows = x_v.shape[0]
    count = rows // TOKENS
    own = count * PK
    keys = far.shape[1]
    chips = n // 2
    me = lax.axis_index("tm")
    core = me % 2
    chip = me // 2
    sibling = chip * 2 + (1 - core)

    blocks = x_sem.shape[0]
    size = rows // blocks
    loads = []
    for b in range(blocks):
        part = pl.ds(b * size, size)
        loads.append(pltpu.make_async_copy(x_hbm.at[part], x_v.at[part], x_sem.at[b]))
        loads[-1].start()
    small = [pltpu.make_async_copy(gain_hbm, gain, small_sem.at[0]), pltpu.make_async_copy(ft_hbm, ft, small_sem.at[1])]
    for copy in small:
        copy.start()
    weights = []
    for i, (src, dst) in enumerate(((wk_hbm, wk), (wv_hbm, wv), (wq_hbm, wq), (wo_hbm, wo))):
        weights.append(pltpu.make_async_copy(src, dst, w_sem.at[i]))
    for copy in weights:
        copy.start()

    plan = (grid_plan if snake else ring_plan)(n, own, cut, core, chip)
    place_of, peers, slots, hop = plan
    barrier = pltpu.get_barrier_semaphore()
    for other in (*peers, sibling):
        pl.semaphore_signal(barrier, inc=1, device_id={"tm": other}, device_id_type=MESH)

    small[0].wait()
    sub = 32
    for b in range(blocks):
        loads[b].wait()

        def norm(i, carry, b=b):
            part = pl.ds(pl.multiple_of(b * size + i * sub, sub), sub)
            xf = x_v[part, :].astype(jnp.float32)
            scale = lax.rsqrt(jnp.mean(xf * xf, axis=-1, keepdims=True) + 1e-06)
            normed[part, :] = (xf * scale * gain[...]).astype(jnp.bfloat16)
            return carry

        lax.fori_loop(0, size // sub, norm, 0)

    pr = lax.broadcasted_iota(jnp.int32, (own, rows), 0)
    pc = lax.broadcasted_iota(jnp.int32, (own, rows), 1)
    block_of = (pc // TOKENS) * PK + (pc % TOKENS) // (POOL * WW) * (WW // POOL) + (pc % WW) // POOL
    pool = jnp.where(pr == block_of, 1.0 / (POOL * POOL), 0.0).astype(jnp.bfloat16)

    sends = []

    def go(copy):
        copy.start()
        sends.append(copy)

    def remote(piece, name):
        src, dst, device, index = hop(name, piece)
        return pltpu.make_async_remote_copy(
            src_ref=far.at[piece, pl.ds(src, own)], dst_ref=far.at[piece, pl.ds(dst, own)],
            send_sem=send_sem.at[piece, index], recv_sem=recv_sem.at[piece, index],
            device_id={"tm": device}, device_id_type=MESH)

    def across(piece, slot):
        return pltpu.make_async_remote_copy(
            src_ref=far.at[piece, pl.ds(place_of(slot, 0), own)], dst_ref=far.at[piece, pl.ds(place_of(slot, 1), own)],
            send_sem=sib_send.at[piece, place_of(slot, 0) // (2 * own)], recv_sem=sib_recv.at[piece, place_of(slot, 0) // (2 * own)],
            device_id={"tm": sibling}, device_id_type=MESH)

    def first_sends(piece):
        for name in first_hops(piece):
            go(remote(piece, name))
        go(across(piece, slots[0][0]))

    def take(piece, name, slot, onward):
        remote(piece, name).wait_recv()
        for other in onward:
            go(remote(piece, other))
        go(across(piece, slot))

    def settle(piece, wanted):
        for slot, _ in slots:
            if (place_of(slot, 0) < cut) == wanted:
                across(piece, slot).wait_recv()

    first_hops, steps = (grid_steps if snake else ring_steps)(n, cut, own, place_of)

    def advance(*names):
        for name in names:
            for step in steps.get(name, ()):
                take(*step)

    means = jnp.dot(pool, normed[...], preferred_element_type=jnp.float32).astype(jnp.bfloat16)
    for piece, weight, w in ((0, weights[0], wk), (1, weights[1], wv)):
        weight.wait()
        far[piece, pl.ds(0, own), :] = jnp.dot(
            means, w[...], preferred_element_type=jnp.float32
        ).astype(jnp.bfloat16)
        if piece == 0:
            pl.semaphore_wait(barrier, len(peers) + 1)
        first_sends(piece)

    def project(w, out):
        out[...] = jnp.dot(normed[...], w[...], preferred_element_type=jnp.float32).astype(jnp.bfloat16)

    project(wk, k_s)
    project(wv, v_s)
    advance(0)
    weights[2].wait()
    project(wq, q_s)
    advance(1)

    small[1].wait()
    slot = lax.broadcasted_iota(jnp.int32, (1, keys), 1) // PK
    key_time = jnp.zeros((1, keys), jnp.int32)
    for name, source in slots:
        for cross in (0, 1):
            plane = core * (1 - cross) + (1 - core) * cross
            dev = source * 2 + plane
            first = place_of(name, cross) // PK
            for f in range(count):
                key_time = jnp.where(slot == first + f, ft[dev * count + f], key_time)
    for f in range(count):
        bias[f] = jnp.where(key_time < ft[me * count + f], 0.0, NEG)

    ir = lax.broadcasted_iota(jnp.int32, (HALF, HALF), 0)
    ic = lax.broadcasted_iota(jnp.int32, (HALF, HALF), 1)
    near_bias = jnp.where((ir // WIN) % 2 == (ic // WIN) % 2, 0.0, NEG)
    rate = LOG2E / HD**0.5
    rest = keys - cut
    ones = jnp.ones((1, HD), jnp.bfloat16)

    def with_ones(v):
        return jnp.concatenate([v, jnp.broadcast_to(ones, v.shape)], axis=1)

    def near_pass(first, count):
        jobs = [(h, block) for h in range(first, first + count) for block in range(rows // HALF)]
        scores = {}
        for h, block in jobs:
            here, cols = pl.ds(block * HALF, HALF), pl.ds(h * HD, HD)
            scores[h, block] = lax.dot_general(q_s[here, cols], k_s[here, cols], NT, preferred_element_type=jnp.float32)
        for h, block in jobs:
            here, cols = pl.ds(block * HALF, HALF), pl.ds(h * HD, HD)
            s = scores[h, block] + near_bias
            top = jnp.broadcast_to(jnp.max(s, -1, keepdims=True), (HALF, HD))
            top_s[h, here, :] = top
            w = jnp.exp2((s - top) * rate).astype(jnp.bfloat16)
            acc_s[h, here, :] = jnp.dot(w, with_ones(v_s[here, cols]), preferred_element_type=jnp.float32)

    def score(lo, size):
        span = pl.ds(lo, size)

        def body(h, carry):
            cols = pl.ds(pl.multiple_of(h * HD, HD), HD)
            s_s[:, pl.ds(0, size)] = lax.dot_general(q_s[:, cols], far[0, span, cols], NT, preferred_element_type=jnp.float32)
            for block in range(rows // HALF):
                here = pl.ds(block * HALF, HALF)
                s = s_s[here, pl.ds(0, size)] + bias[block * HALF // TOKENS, :, span]
                old = top_s[h, here, :]
                top = jnp.maximum(old, jnp.broadcast_to(jnp.max(s, -1, keepdims=True), (HALF, HD)))
                keep = jnp.exp2((old - top) * rate)
                acc_s[h, here, :] = acc_s[h, here, :] * jnp.tile(keep, (1, 2))
                if lo == 0:
                    top_s[h, here, :] = top
                w = jnp.exp2((s - jnp.tile(top, (1, -(-size // HD)))[:, :size]) * rate)
                p_all[h, here, span] = w.astype(jnp.bfloat16)
            return carry

        return body

    def sum_first(h, carry):
        cols = pl.ds(pl.multiple_of(h * HD, HD), HD)
        span = pl.ds(0, cut)
        acc = jnp.dot(p_all[h, :, span], with_ones(far[1, span, cols]), preferred_element_type=jnp.float32)
        acc_s[h] = acc_s[h] + acc
        return carry

    def sum_rest(h, carry):
        cols = pl.ds(pl.multiple_of(h * HD, HD), HD)
        span = pl.ds(cut, rest)
        acc = jnp.dot(p_all[h, :, span], with_ones(far[1, span, cols]), preferred_element_type=jnp.float32)
        acc = acc + acc_s[h]
        mixed[:, cols] = (acc[:, :HD] / acc[:, HD:]).astype(jnp.bfloat16)
        return carry

    def over(body, name, parts):
        for part in range(parts):
            lax.fori_loop(part * HEADS // parts, (part + 1) * HEADS // parts, body, 0)
            advance(name + part)

    half = HEADS // 2
    for part in range(2):
        near_pass(part * half, half)
        advance(2 + part)
    settle(0, True)
    over(score(0, cut), 4, 3)
    settle(1, True)
    lax.fori_loop(0, HEADS, sum_first, 0)
    advance(7)
    settle(0, False)
    over(score(cut, rest), 8, 2)
    settle(1, False)
    lax.fori_loop(0, HEADS, sum_rest, 0)
    for copy in sends:
        copy.wait_send()
    weights[3].wait()


def flip(z, k):
    out = z
    bit = 1
    while bit <= k:
        if k // bit % 2:
            out = out + bit - 2 * bit * (z // bit % 2)
        bit *= 2
    return out


def grid_plan(n, own, cut, core, chip):
    deep = n // 4
    y = chip % 2
    z = chip // 2

    def place_of(slot, cross):
        k, f = slot
        return (4 * k + 2 * f + cross) * own

    def device(k, f):
        side = y if f == 0 else 1 - y
        return (flip(z, k) * 2 + side) * 2 + core

    def hop(name, piece):
        kind, k = name
        if kind == "z":
            return place_of((0, 0), 0), place_of((k, 0), 0), device(k, 0), k
        return place_of((k, 0), 0), place_of((k, 1), 0), device(0, 1), deep + k

    peers = [device(k, 0) for k in range(1, deep)] + [device(0, 1)]
    slots = [((k, f), device(k, f) // 2) for k in range(deep) for f in (0, 1)]
    return place_of, peers, slots, hop


def grid_steps(n, cut, own, place_of):
    deep = n // 4
    inner = [k for k in range(1, deep) if place_of((k, 0), 0) < cut]
    outer = [k for k in range(1, deep) if place_of((k, 0), 0) >= cut]

    def first_hops(piece):
        return [("z", k) for k in range(1, deep)] + [("y", 0)]

    def from_z(piece, ks):
        return [(piece, ("z", k), (k, 0), [("y", k)]) for k in ks]

    def from_y(piece, ks):
        return [(piece, ("y", k), (k, 1), []) for k in ks]

    steps = {
        0: from_z(0, inner) + from_y(0, [0]),
        1: from_z(1, inner) + from_y(1, [0]),
        2: from_z(0, outer[:1]),
        3: from_z(0, outer[1:]) + from_y(0, inner),
        4: from_z(1, outer[:1]),
        5: from_y(1, inner),
        6: from_z(1, outer[1:]),
        7: from_y(0, outer),
        9: from_y(1, outer),
    }
    return first_hops, steps


def ring_plan(n, own, cut, core, chip):
    chips = n // 2

    def place_of(slot, cross):
        way, dist = slot
        if dist == 0:
            return cross * own
        first = (4 * dist - 2) * own
        if 2 * dist == chips:
            return first + cross * own
        return first + (2 * way + cross) * own

    def chip_at(way, dist):
        return (chip + (1, -1)[way] * dist + chips) % chips

    def hop(name, piece):
        way, dist = name
        return place_of((way, dist - 1), 0), place_of((way, dist), 0), chip_at(way, 1) * 2 + core, way * (chips // 2) + dist - 1

    peers = [chip_at(way, 1) * 2 + core for way in (0, 1)]
    slots = [((0, 0), chip)]
    for dist in range(1, chips // 2 + 1):
        for way in (0, 1) if 2 * dist < chips else (0,):
            slots.append(((way, dist), chip_at(1 - way, dist)))
    return place_of, peers, slots, hop


def ring_steps(n, cut, own, place_of):
    chips = n // 2
    reach = (chips // 2, (chips - 1) // 2)

    def limit(way, piece):
        return reach[way] if piece == 0 else reach[1 - way]

    def first_hops(piece):
        return [(way, 1) for way in (0, 1) if limit(way, piece) >= 1]

    steps = {3: [], 7: []}
    for dist in range(1, reach[0] + 1):
        early = place_of((0, dist), 0) < cut
        for piece in (0, 1):
            name = 3 if early else 7
            for way in (0, 1):
                if dist <= limit(way, piece):
                    onward = [(way, dist + 1)] if dist < limit(way, piece) else []
                    slot = (0, dist) if 2 * dist == chips else (way, dist)
                    steps[name].append((piece, (way, dist), slot, onward))
    return first_hops, steps


def finish(mixed, wo, out_hbm, out_v, sem):
    chunks, rows, width = out_v.shape
    copies = []
    for c in range(chunks):
        cols = pl.ds(c * width, width)
        out_v[c] = jnp.dot(mixed[...], wo[:, cols], preferred_element_type=jnp.float32).astype(jnp.bfloat16)
        copies.append(pltpu.make_async_copy(out_v.at[c], out_hbm.at[:, cols], sem.at[c]))
        copies[-1].start()
    for copy in copies:
        copy.wait()


def on_device(n, snake, frames_in, frame_time, norm_gain, w_query, w_key, w_value, w_output):
    rows, width = frames_in.shape
    inner = w_query.shape[1]
    count = rows // TOKENS
    keys = n * count * PK
    slots = n // 2
    half = keys // 2
    cut = half if snake else half + 2 * count * PK
    bf = jnp.bfloat16
    f32 = jnp.float32
    dma = pltpu.SemaphoreType.DMA
    hbm = pl.BlockSpec(memory_space=pl.ANY)
    vmem = pl.BlockSpec(memory_space=pltpu.VMEM)
    mixed, wo = pl.pallas_call(
        functools.partial(kernel, n, snake, cut),
        out_shape=(pltpu.VMEM((rows, inner), bf), pltpu.VMEM((inner, width), bf)),
        in_specs=[hbm, hbm, hbm, hbm, hbm, hbm, hbm],
        out_specs=(vmem, vmem),
        scratch_shapes=[
            pltpu.SMEM(frame_time.shape, jnp.int32),
            pltpu.VMEM(norm_gain.shape, f32),
            pltpu.VMEM((rows, width), bf),
            pltpu.VMEM((width, inner), bf),
            pltpu.VMEM((width, inner), bf),
            pltpu.VMEM((width, inner), bf),
            pltpu.VMEM((rows, width), bf),
            pltpu.VMEM((rows, inner), bf),
            pltpu.VMEM((rows, inner), bf),
            pltpu.VMEM((rows, inner), bf),
            pltpu.VMEM((2, keys, inner), bf),
            pltpu.VMEM((count, 1, keys), f32),
            pltpu.VMEM((HEADS, rows, HD), f32),
            pltpu.VMEM((HEADS, rows, 2 * HD), f32),
            pltpu.VMEM((rows, cut), f32),
            pltpu.VMEM((HEADS, rows, keys), bf),
            dma((4,)),
            dma((4,)),
            dma((2,)),
            dma((2, slots)),
            dma((2, slots)),
            dma((2, slots)),
            dma((2, slots)),
        ],
        compiler_params=pltpu.CompilerParams(
            collective_id=0, has_side_effects=True, vmem_limit_bytes=60 << 20
        ),
    )(frame_time, norm_gain, frames_in, w_query, w_key, w_value, w_output)
    chunks = width // (4 * HD)
    return pl.pallas_call(
        finish,
        out_shape=jax.ShapeDtypeStruct((rows, width), bf),
        in_specs=[vmem, vmem],
        out_specs=hbm,
        scratch_shapes=[pltpu.VMEM((chunks, rows, width // chunks), bf), dma((chunks,))],
        compiler_params=pltpu.CompilerParams(vmem_limit_bytes=8 << 20),
    )(mixed, wo)


def is_snake(mesh):
    names = list(mesh.axis_names)
    line = mesh.devices.transpose(names.index("grp"), names.index("tm"))[0]
    try:
        second = {d.coords[1] for d in line}
        third = {d.coords[2] for d in line}
    except (AttributeError, TypeError):
        return False
    deep = len(third)
    return len(second) == 2 and deep * 4 == len(line) and deep in [2**k for k in range(deep)]


def solution(mesh):
    placed = (P(("grp", "tm"), None), P("grp"), P(), P(), P(), P(), P())
    n = mesh.shape["tm"]
    return jax.shard_map(
        functools.partial(on_device, n, is_snake(mesh)),
        mesh=mesh, in_specs=placed, out_specs=P(("grp", "tm"), None), check_vma=False,
    )
```

time: 33 us -> 31.7 us (0.961)
  Pallas kernels: 32.4 us -> 31.1 us
    pallas_call x1, Pallas kernels: 30.2 us -> 28.9 us  [on_device(): pl.pallas_call(functools.partial(kernel, n, snake, cut), out_shape=(pltpu...]
where the time goes in v2:
time: 31.7 us; the launch traced here: 31.1 us
  Pallas kernels  31.1 us (98%)
    pallas_call x1, Pallas kernels, on_device(): pl.pallas_call(functools.partial(kernel, n, snake, cut), out_shape=(pltpu...  28.9 us
    pallas_call x1, Pallas kernels, on_device(): pl.pallas_call(finish, out_shape=jax.ShapeDtypeStruct((rows, width), bf),...  2.21 us

profile of v2, /device:TPU:1, one launch (start us, length us, event | category | flops | bytes accessed | tf_op | source)
XLA Modules:
  0.0 31.1 jit_solution(412555534818474121)
XLA Ops:
  0.0 28.9 %shard_map.73 = (bf16[512,768]{1,0:T(8,128)(2,1)S(1)}, bf16[768,1536]{1,0:T(8,128)(2,1)S(1)}) custom-call(s32[32]{0:T(128)} %ft_hbm.1, f32[1536]{0:T(1024)} %gain_hbm.1, bf16[512,1536]{1,0:T(8,128)(2,1)} %x_hbm.1, bf16[1536,768]{1,0:T(8,128)(2,1)} %wq_hbm.1, bf16[1536,768]{1,0:T(8,128)(2,1)} %wk_hbm.1, bf16[1536,768]{1,0:T(8,128)(2,1)} %wv_hbm.1, ...), custom_call_target="tpu_custom_call" | custom-call | tf_op jit(solution)/shard_map/pallas_call | solution.py:374
  28.9 2.2 %shard_map.74 = bf16[512,1536]{1,0:T(8,128)(2,1)} custom-call(bf16[512,768]{1,0:T(8,128)(2,1)S(1)} %get-tuple-element.7.mixed, bf16[768,1536]{1,0:T(8,128)(2,1)S(1)} %get-tuple-element.8.wo), custom_call_target="tpu_custom_call" | custom-call | tf_op jit(solution)/shard_map/pallas_call | solution.py:409
